TPU v7x, 128 devices: a whole 4x4x4 slice. The times are simulated.
128 devices in a mesh: group: 8 (over y, core), within: 16 (over z, x).
Axes of the slice: x: 4, y: 4, z: 4, core: 2. Of those that a mesh axis runs over, the one named last changes fastest.
Arguments:
- tokens: bfloat16 [16384, 2048], P(('group', 'within')), may hold values from -6 to 6
- languages: int32 [16384], P(('group', 'within')), may hold values from 0 to 99, as said below
- lang_group: int32 [100], replicated, may hold values from 0 to 7, as said below
- group_gain: float32 [8, 2048], replicated, may hold values from 0.25 to 1.75
- group_w1: bfloat16 [8, 2048, 8192], P('group', None, 'within'), may hold values from -0.125 to 0.125
- group_b1: float32 [8, 8192], P('group', 'within'), may hold values from -3 to 3
- group_w2: bfloat16 [8, 8192, 2048], P('group', 'within'), may hold values from -0.0625 to 0.0625
- group_b2: float32 [8, 2048], replicated, may hold values from -3 to 3
- shared_gain: float32 [2048], replicated, may hold values from 0.25 to 1.75
- shared_w1: bfloat16 [2048, 8192], P(None, 'group'), may hold values from -0.125 to 0.125
- shared_b1: float32 [8192], P('group'), may hold values from -3 to 3
- shared_w2: bfloat16 [8192, 2048], P('group'), may hold values from -0.0625 to 0.0625
- shared_b2: float32 [2048], replicated, may hold values from -3 to 3
Outputs:
- encoded: bfloat16 [16384, 2048], P(('group', 'within'))
Inputs may be any that keep to these rules, and one draw needn't show every extreme that they name: `lang_group`: every language lies in one group and every group holds at least one language. Among the 128 tokens of one device (an aligned block), at most 24 have languages of one group, and in every block some group has exactly 24.
All inputs are finite; a program needn't handle non-finite values.
Results may differ from a plain program's by a relative error of at most 0.017.
Values may be sent and summed in bfloat16 or wider, within the bound.
No kernel may reach another device: no remote copies, remote signals or barrier semaphores. Data moves between devices by JAX's collectives and lax.ppermute only.
A program may use at most 128 MiB of HBM per device.

v0:
```python
import jax
import jax.numpy as jnp
from jax import lax
from jax.sharding import PartitionSpec as P


def layer_norm(values, gains):
    centre = jnp.mean(values, axis=-1, keepdims=True)
    centred = values - centre
    spread = jnp.mean(centred * centred, axis=-1, keepdims=True)
    return centred * lax.rsqrt(spread + 1e-05) * gains


def on_device(
    tokens,
    languages,
    lang_group,
    group_gain,
    group_w1,
    group_b1,
    group_w2,
    group_b2,
    shared_gain,
    shared_w1,
    shared_b1,
    shared_w2,
    shared_b2,
):
    tok_dev = tokens.shape[0]
    width_model = tokens.shape[1]
    num_groups = group_gain.shape[0]
    num_langs = lang_group.shape[0]
    capacity = 3 * tok_dev // (2 * lax.axis_size("group"))
    residual_in = tokens.astype(jnp.float32)
    lang_hit = (languages[:, None] == jnp.arange(num_langs, dtype=jnp.int32)[None, :]).astype(
        jnp.int32
    )
    group_of = jnp.sum(lang_hit * lang_group[None, :], axis=1)
    onehot = (group_of[:, None] == jnp.arange(num_groups, dtype=jnp.int32)[None, :]).astype(
        jnp.int32
    )
    earlier = jnp.cumsum(onehot, axis=0) - onehot
    slot_index = jnp.sum(earlier * onehot, axis=1)
    position = group_of * capacity + slot_index
    dispatch_map = (
        position[None, :] == jnp.arange(num_groups * capacity, dtype=jnp.int32)[:, None]
    ).astype(jnp.bfloat16)
    onehot_float = onehot.astype(jnp.float32)
    row_gains = jnp.dot(onehot_float, group_gain, precision=lax.Precision.HIGHEST)
    normed = layer_norm(residual_in, row_gains).astype(jnp.bfloat16)
    outgoing = jnp.dot(dispatch_map, normed, preferred_element_type=jnp.float32).astype(
        jnp.bfloat16
    )
    outgoing = outgoing.reshape(num_groups, capacity, width_model)
    arrived = lax.all_to_all(outgoing, "group", split_axis=0, concat_axis=0, tiled=True)
    group_rows = arrived.reshape(num_groups * capacity, width_model)
    first_proj = group_w1[0]
    first_bias = group_b1[0]
    second_proj = group_w2[0]
    hidden = jax.nn.relu(
        jnp.dot(
            lax.all_gather(group_rows, "within", axis=0, tiled=True),
            first_proj,
            preferred_element_type=jnp.float32,
        )
        + first_bias
    ).astype(jnp.bfloat16)
    selected = hidden
    summed = lax.psum_scatter(
        jnp.dot(selected, second_proj, preferred_element_type=jnp.float32).astype(jnp.bfloat16),
        "within",
        scatter_dimension=0,
        tiled=True,
    )
    returned = lax.all_to_all(
        summed.reshape(num_groups, capacity, width_model),
        "group",
        split_axis=0,
        concat_axis=0,
        tiled=True,
    )
    returned = returned.reshape(num_groups * capacity, width_model)
    group_out = lax.dot_general(
        dispatch_map, returned, (((0,), (0,)), ((), ())), preferred_element_type=jnp.float32
    )
    group_bias = jnp.dot(onehot_float, group_b2, precision=lax.Precision.HIGHEST)
    middle = residual_in + group_out + group_bias
    shared_in = layer_norm(middle, shared_gain).astype(jnp.bfloat16)
    shared_hidden = jax.nn.relu(
        jnp.dot(
            lax.all_gather(shared_in, "group", axis=0, tiled=True),
            shared_w1,
            preferred_element_type=jnp.float32,
        )
        + shared_b1
    ).astype(jnp.bfloat16)
    selected = shared_hidden
    shared_out = lax.psum_scatter(
        jnp.dot(selected, shared_w2, preferred_element_type=jnp.float32).astype(jnp.bfloat16),
        "group",
        scatter_dimension=0,
        tiled=True,
    ).astype(jnp.float32)
    return (middle + shared_out + shared_b2).astype(jnp.bfloat16)


def solution(mesh):
    placed = (
        P(("group", "within"), None),
        P(("group", "within")),
        P(),
        P(),
        P("group", None, "within"),
        P("group", "within"),
        P("group", "within", None),
        P(),
        P(),
        P(None, "group"),
        P("group"),
        P("group", None),
        P(),
    )
    return jax.shard_map(
        on_device,
        mesh=mesh,
        in_specs=placed,
        out_specs=P(("group", "within"), None),
        check_vma=False,
    )
```

profile of v0, /device:TPU:0, one launch (start us, length us, event | category | flops | bytes accessed | tf_op | source)
XLA Modules:
  0.0 346.0 jit_solution(16796450870467543149)
XLA Ops:
  6.5 0.0 copy-start
  6.5 0.0 copy-start.6
  6.5 0.0 all-gather.3.cloned.1.call-start
  6.5 1.3 convert_reduce_fusion
  7.9 1.3 fusion.10
  9.2 0.8 select_reduce_fusion
  10.0 0.1 fusion.17
  10.1 0.2 reduce_window_sum.11
  10.3 0.2 fusion.16
  10.5 2.2 fusion
  12.6 0.4 convolution_convert_fusion.2
  13.0 17.7 %all_to_all.10 = bf16[8,24,2048]{2,1,0:T(8,128)(2,1)} all-to-all(bf16[8,24,2048]{2,1,0:T(8,128)(2,1)S(1)} %bitcast.22), channel_id=1, replica_groups=mesh['group'=8,'within'=16] {'group'}, dimensions={0} | all-to-all | bytes 1572864 | tf_op jit(solution)/shard_map/all_to_all | solution.py:55
  30.7 0.0 all-gather.3.cloned.1.call-update
  30.7 0.0 reduce-scatter.3.cloned.1.call-start
  30.8 90.6 %all-gather.3.cloned.1.call-done = bf16[3072,2048]{1,0:T(8,128)(2,1)} async-done(((bf16[192,2048]{1,0:T(8,128)(2,1)}), bf16[3072,2048]{1,0:T(8,128)(2,1)}) %all-gather.3.cloned.1.call-update) | async-done | bytes 12582928 | tf_op jit(solution)/shard_map/all_gather | solution.py:62
  121.4 0.0 copy-done
  121.4 0.0 copy-done.6
  121.4 19.5 %convolution_convert_fusion = bf16[3072,2048]{1,0:T(8,128)(2,1)} fusion(bf16[1,512,2048]{2,1,0:T(8,128)(2,1)S(1)} %copy-done, bf16[3072,2048]{1,0:T(8,128)(2,1)} %all-gather.3.cloned.1.call-done, f32[512]{0:T(512)S(1)} %bitcast.24, bf16[1,2048,512]{2,1,0:T(8,128)(2,1)} %param.17), kind=kOutput, calls=%fused_computation | convolution fusion | flops 12895911936 | bytes 29362176 | tf_op jit(solution)/shard_map/dot_general | solution.py:70
  140.8 0.0 copy-start.1
  140.8 0.0 copy-start.2
  140.8 0.0 reduce-scatter.3.cloned.1.call-update
  140.9 0.0 copy-start.3
  140.9 0.0 all-gather.5.cloned.1.call-start
  140.9 94.3 %reduce-scatter.3.cloned.1.call-done = bf16[192,2048]{1,0:T(8,128)(2,1)} async-done(((bf16[3072,2048]{1,0:T(8,128)(2,1)}), bf16[192,2048]{1,0:T(8,128)(2,1)}) %reduce-scatter.3.cloned.1.call-update) | async-done | bytes 786448 | tf_op jit(solution)/shard_map/reduce_scatter | solution.py:69
  235.2 17.5 %all_to_all.11 = bf16[8,24,2048]{2,1,0:T(8,128)(2,1)S(1)} all-to-all(bf16[8,24,2048]{2,1,0:T(8,128)(2,1)} %bitcast.23), channel_id=1, replica_groups=mesh['group'=8,'within'=16] {'group'}, dimensions={0} | all-to-all | bytes 1572864 | tf_op jit(solution)/shard_map/all_to_all | solution.py:75
  252.7 0.0 copy-start.5
  252.7 0.0 copy-done.1
  252.7 0.4 convolution_add_fusion.1
  253.1 0.0 copy-done.2
  253.1 1.1 fusion.24
  254.3 0.3 multiply_reduce_fusion
  254.5 0.0 copy-done.3
  254.5 1.0 multiply_convert_fusion
  255.5 0.0 all-gather.5.cloned.1.call-update
  255.6 0.2 reduce-scatter.5.cloned.1.call-start
  255.8 29.2 %all-gather.5.cloned.1.call-done = bf16[1024,2048]{1,0:T(8,128)(2,1)} async-done(((bf16[128,2048]{1,0:T(8,128)(2,1)}), bf16[1024,2048]{1,0:T(8,128)(2,1)}) %all-gather.5.cloned.1.call-update) | async-done | bytes 4194320 | tf_op jit(solution)/shard_map/all_gather | solution.py:91
  285.0 0.0 copy-done.5
  285.0 14.3 %convolution_convert_fusion.1 = bf16[1024,2048]{1,0:T(8,128)(2,1)} fusion(bf16[1024,2048]{1,0:T(8,128)(2,1)} %param.24, f32[1024]{0:T(1024)S(1)} %copy-done.5, bf16[1024,2048]{1,0:T(8,128)(2,1)} %all-gather.5.cloned.1.call-done, bf16[2048,1024]{1,0:T(8,128)(2,1)} %param.22), kind=kOutput, calls=%fused_computation.3 | convolution fusion | flops 8595177472 | bytes 16781312 | tf_op jit(solution)/shard_map/dot_general | solution.py:99
  299.3 0.0 copy-start.4
  299.3 0.0 reduce-scatter.5.cloned.1.call-update
  299.4 38.1 %reduce-scatter.5.cloned.1.call-done = bf16[128,2048]{1,0:T(8,128)(2,1)} async-done(((bf16[1024,2048]{1,0:T(8,128)(2,1)}), bf16[128,2048]{1,0:T(8,128)(2,1)}) %reduce-scatter.5.cloned.1.call-update) | async-done | bytes 524304 | tf_op jit(solution)/shard_map/reduce_scatter | solution.py:98
  337.5 0.0 copy-done.4
  337.5 2.0 add_convert_fusion
  (5 shorter events, 0.0 us)
Async XLA Ops:
  6.5 114.8 %copy-start = (bf16[1,512,2048]{2,1,0:T(8,128)(2,1)S(1)}, bf16[1,512,2048]{2,1,0:T(8,128)(2,1)}, u32[]{:S(2)}) copy-start(bf16[1,512,2048]{2,1,0:T(8,128)(2,1)} %param.19) | copy-start | bytes 6291460
  6.5 114.8 %copy-start.6 = (f32[1,512]{1,0:T(1,128)S(1)}, f32[1,512]{1,0:T(1,128)}, u32[]{:S(2)}) copy-start(f32[1,512]{1,0:T(1,128)} %param.18) | copy-start | bytes 6148
  6.5 114.8 %all-gather.3.cloned.1.call-start = ((), (), s32[]{:S(2)}) async-start(), calls=%async_computation.4 | async-start | bytes 13369344 | tf_op jit(solution)/shard_map/all_gather | solution.py:62
  30.7 204.5 %reduce-scatter.3.cloned.1.call-start = ((), (), s32[]{:S(2)}) async-start(), calls=%async_computation.5 | async-start | bytes 13369344 | tf_op jit(solution)/shard_map/reduce_scatter | solution.py:69
  140.8 111.9 %copy-start.1 = (bf16[128,2048]{1,0:T(8,128)(2,1)S(1)}, bf16[128,2048]{1,0:T(8,128)(2,1)}, u32[]{:S(2)}) copy-start(bf16[128,2048]{1,0:T(8,128)(2,1)} %param.13) | copy-start | bytes 1572868
  140.8 112.3 %copy-start.2 = (f32[8,2048]{1,0:T(8,128)S(1)}, f32[8,2048]{1,0:T(8,128)}, u32[]{:S(2)}) copy-start(f32[8,2048]{1,0:T(8,128)} %param.20) | copy-start | bytes 196612
  140.9 113.7 %copy-start.3 = (f32[2048]{0:T(1024)S(1)}, f32[2048]{0:T(1024)}, u32[]{:S(2)}) copy-start(f32[2048]{0:T(1024)} %param.21) | copy-start | bytes 24580
  140.9 144.1 %all-gather.5.cloned.1.call-start = ((), (), s32[]{:S(2)}) async-start(), calls=%async_computation.6 | async-start | bytes 4718592 | tf_op jit(solution)/shard_map/all_gather | solution.py:91
  252.7 32.3 %copy-start.5 = (f32[1024]{0:T(1024)S(1)}, f32[1024]{0:T(1024)}, u32[]{:S(2)}) copy-start(f32[1024]{0:T(1024)} %param.23) | copy-start | bytes 12292
  255.6 81.9 %reduce-scatter.5.cloned.1.call-start = ((), (), s32[]{:S(2)}) async-start(), calls=%async_computation.7 | async-start | bytes 4718592 | tf_op jit(solution)/shard_map/reduce_scatter | solution.py:98
  299.3 38.1 %copy-start.4 = (f32[2048]{0:T(1024)S(1)}, f32[2048]{0:T(1024)}, u32[]{:S(2)}) copy-start(f32[2048]{0:T(1024)} %param.25) | copy-start | bytes 24580
Sparse Core Ops, SparseCore 0:
  30.8 90.4 all-gather.2
  141.0 94.1 reduce-scatter.2
  255.7 29.2 all-gather.4
  299.5 37.9 reduce-scatter.4
where the time goes:
time: 346 us
  waiting for transfers between devices  252 us (73%)
  matrix products  37.8 us (11%)
  blocking collectives  35.2 us (10%)
  between operations  13.2 us (4%)
  other arithmetic  7.17 us (2%)
    reduce_scatter x1, waiting for transfers between devices, on_device(): lax.psum_scatter(jnp.dot(selected, second_proj, preferred_element_type=jn...  94.3 us
    all_gather x1, waiting for transfers between devices, on_device(): lax.all_gather(group_rows, 'within', axis=0, tiled=True)  90.6 us
    reduce_scatter x1, waiting for transfers between devices, on_device(): lax.psum_scatter(jnp.dot(selected, shared_w2, preferred_element_type=jnp....  38.1 us
    all_gather x1, waiting for transfers between devices, on_device(): lax.all_gather(shared_in, 'group', axis=0, tiled=True)  29.2 us
    dot_general x1, matrix products, on_device(): jnp.dot(selected, second_proj, preferred_element_type=jnp.float32)  19.5 us
    all_to_all x1, blocking collectives, on_device(): lax.all_to_all(outgoing, 'group', split_axis=0, concat_axis=0, tiled=True)  17.7 us
    all_to_all x1, blocking collectives, on_device(): lax.all_to_all(summed.reshape(num_groups, capacity, width_model), 'group'...  17.5 us
    dot_general x1, matrix products, on_device(): jnp.dot(selected, shared_w2, preferred_element_type=jnp.float32)  14.3 us
  transfers between devices with their start and end apart: 4, of which 4 were waited for; matrix products, arithmetic and copies ran while one was open for 0% of the time, Pallas kernels for 0%

commit v1 on v0

--- a/solution.py
+++ b/solution.py
@@ -59,7 +59,10 @@
     second_proj = group_w2[0]
     hidden = jax.nn.relu(
         jnp.dot(
-            lax.all_gather(group_rows, "within", axis=0, tiled=True),
+            jnp.concatenate(
+                lax.all_to_all(jnp.stack([group_rows] * lax.axis_size("within")), "within", 0, 0),
+                axis=0,
+            ),
             first_proj,
             preferred_element_type=jnp.float32,
         )

time: 346 us -> 406 us (1.17)
  blocking collectives: 35.2 us -> 184 us
  waiting for transfers between devices: 252 us -> 158 us
  local copies, waits for them, and re-layouts: 0.03 us -> 6.13 us
    all_to_all x0 -> x1, blocking collectives: none -> 148 us  [on_device(): lax.all_to_all(jnp.stack([group_rows] * lax.axis_size('within')), 'within...]
    all_gather x1 -> x0, waiting for transfers between devices: 90.6 us -> none  [on_device(): lax.all_gather(group_rows, 'within', axis=0, tiled=True)]
    another operation x0 -> x1, local copies, waits for them, and re-layouts: none -> 6.11 us  [on_device(): jnp.stack([group_rows] * lax.axis_size('within'))]
  transfers between devices with their start and end apart: 4 -> 3, of which waited for: 4 -> 3; matrix products, arithmetic and copies ran while one was open for 0% -> 0% of each run, Pallas kernels for 0% -> 0%
where the time goes in v1:
time: 406 us
  blocking collectives  184 us (45%)
  waiting for transfers between devices  158 us (39%)
  matrix products  37.8 us (9%)
  between operations  13.2 us (3%)
  other arithmetic  7.17 us (2%)
  local copies, waits for them, and re-layouts  6.13 us (2%)
    all_to_all x1, blocking collectives, on_device(): lax.all_to_all(jnp.stack([group_rows] * lax.axis_size('within')), 'within...  148 us
    reduce_scatter x1, waiting for transfers between devices, on_device(): lax.psum_scatter(jnp.dot(selected, second_proj, preferred_element_type=jn...  90.2 us
    reduce_scatter x1, waiting for transfers between devices, on_device(): lax.psum_scatter(jnp.dot(selected, shared_w2, preferred_element_type=jnp....  38.1 us
    all_gather x1, waiting for transfers between devices, on_device(): lax.all_gather(shared_in, 'group', axis=0, tiled=True)  29.2 us
    dot_general x1, matrix products, on_device(): jnp.dot(selected, second_proj, preferred_element_type=jnp.float32)  19.5 us
    all_to_all x1, blocking collectives, on_device(): lax.all_to_all(outgoing, 'group', split_axis=0, concat_axis=0, tiled=True)  17.6 us
    all_to_all x1, blocking collectives, on_device(): lax.all_to_all(summed.reshape(num_groups, capacity, width_model), 'group'...  17.5 us
    dot_general x1, matrix products, on_device(): jnp.dot(selected, shared_w2, preferred_element_type=jnp.float32)  14.3 us
  transfers between devices with their start and end apart: 3, of which 3 were waited for; matrix products, arithmetic and copies ran while one was open for 0% of the time, Pallas kernels for 0%

profile of v1, /device:TPU:0, one launch (start us, length us, event | category | flops | bytes accessed | tf_op | source)
XLA Modules:
  0.0 405.7 jit_solution(15099694195227286851)
XLA Ops:
  6.5 0.0 copy-start
  6.5 0.0 reduce-scatter.3.cloned.1.call-start
  6.5 1.3 convert_reduce_fusion
  7.9 1.3 fusion.10
  9.2 0.8 select_reduce_fusion
  10.0 0.1 fusion.17
  10.1 0.2 reduce_window_sum.11
  10.3 0.2 fusion.16
  10.5 2.2 fusion
  12.6 0.4 convolution_convert_fusion.2
  13.0 17.6 %all_to_all.15 = bf16[8,24,2048]{2,1,0:T(8,128)(2,1)S(1)} all-to-all(bf16[8,24,2048]{2,1,0:T(8,128)(2,1)S(1)} %bitcast.24), channel_id=1, replica_groups=mesh['group'=8,'within'=16] {'group'}, dimensions={0} | all-to-all | bytes 1572864 | tf_op jit(solution)/shard_map/all_to_all | solution.py:55
  30.6 6.1 %stack.3 = bf16[16,192,2048]{2,1,0:T(8,128)(2,1)} broadcast(bf16[192,2048]{1,0:T(8,128)(2,1)S(1)} %bitcast.23), dimensions={1,2} | broadcast | bytes 13369344 | tf_op jit(solution)/shard_map/stack | solution.py:63
  36.7 0.0 copy-start.6
  36.7 148.5 %all_to_all.16 = bf16[16,192,2048]{2,1,0:T(8,128)(2,1)} all-to-all(bf16[16,192,2048]{2,1,0:T(8,128)(2,1)} %stack.3), channel_id=1, replica_groups=mesh['group'=8,'within'=16] {'within'}, dimensions={0} | all-to-all | bytes 25165824 | tf_op jit(solution)/shard_map/all_to_all | solution.py:63
  185.2 0.0 copy-done
  185.2 0.0 copy-done.6
  185.2 19.5 %convolution_convert_fusion = bf16[3072,2048]{1,0:T(8,128)(2,1)} fusion(bf16[1,512,2048]{2,1,0:T(8,128)(2,1)S(1)} %copy-done, bf16[3072,2048]{1,0:T(8,128)(2,1)} %bitcast.21, f32[512]{0:T(512)S(1)} %bitcast.26, bf16[1,2048,512]{2,1,0:T(8,128)(2,1)} %param.17), kind=kOutput, calls=%fused_computation | convolution fusion | flops 12895911936 | bytes 29362176 | tf_op jit(solution)/shard_map/dot_general | solution.py:73
  204.6 0.0 copy-start.1
  204.7 0.0 copy-start.2
  204.7 0.0 reduce-scatter.3.cloned.1.call-update
  204.7 0.0 copy-start.3
  204.7 0.0 all-gather.2.cloned.1.call-start
  204.7 90.2 %reduce-scatter.3.cloned.1.call-done = bf16[192,2048]{1,0:T(8,128)(2,1)} async-done(((bf16[3072,2048]{1,0:T(8,128)(2,1)}), bf16[192,2048]{1,0:T(8,128)(2,1)}) %reduce-scatter.3.cloned.1.call-update) | async-done | bytes 786448 | tf_op jit(solution)/shard_map/reduce_scatter | solution.py:72
  294.9 17.5 %all_to_all.17 = bf16[8,24,2048]{2,1,0:T(8,128)(2,1)S(1)} all-to-all(bf16[8,24,2048]{2,1,0:T(8,128)(2,1)} %bitcast.25), channel_id=1, replica_groups=mesh['group'=8,'within'=16] {'group'}, dimensions={0} | all-to-all | bytes 1572864 | tf_op jit(solution)/shard_map/all_to_all | solution.py:78
  312.5 0.0 copy-start.5
  312.5 0.0 copy-done.1
  312.5 0.4 convolution_add_fusion.1
  312.8 0.0 copy-done.2
  312.8 1.1 fusion.24
  314.0 0.3 multiply_reduce_fusion
  314.3 0.0 copy-done.3
  314.3 1.0 multiply_convert_fusion
  315.3 0.0 all-gather.2.cloned.1.call-update
  315.3 0.2 reduce-scatter.5.cloned.1.call-start
  315.5 29.2 %all-gather.2.cloned.1.call-done = bf16[1024,2048]{1,0:T(8,128)(2,1)} async-done(((bf16[128,2048]{1,0:T(8,128)(2,1)}), bf16[1024,2048]{1,0:T(8,128)(2,1)}) %all-gather.2.cloned.1.call-update) | async-done | bytes 4194320 | tf_op jit(solution)/shard_map/all_gather | solution.py:94
  344.7 0.0 copy-done.5
  344.7 14.3 %convolution_convert_fusion.1 = bf16[1024,2048]{1,0:T(8,128)(2,1)} fusion(bf16[1024,2048]{1,0:T(8,128)(2,1)} %param.24, f32[1024]{0:T(1024)S(1)} %copy-done.5, bf16[1024,2048]{1,0:T(8,128)(2,1)} %all-gather.2.cloned.1.call-done, bf16[2048,1024]{1,0:T(8,128)(2,1)} %param.22), kind=kOutput, calls=%fused_computation.3 | convolution fusion | flops 8595177472 | bytes 16781312 | tf_op jit(solution)/shard_map/dot_general | solution.py:102
  359.1 0.0 copy-start.4
  359.1 0.0 reduce-scatter.5.cloned.1.call-update
  359.1 38.1 %reduce-scatter.5.cloned.1.call-done = bf16[128,2048]{1,0:T(8,128)(2,1)} async-done(((bf16[1024,2048]{1,0:T(8,128)(2,1)}), bf16[128,2048]{1,0:T(8,128)(2,1)}) %reduce-scatter.5.cloned.1.call-update) | async-done | bytes 524304 | tf_op jit(solution)/shard_map/reduce_scatter | solution.py:101
  397.2 0.0 copy-done.4
  397.2 2.0 add_convert_fusion
  (5 shorter events, 0.0 us)
Async XLA Ops:
  6.5 178.7 %copy-start = (bf16[1,512,2048]{2,1,0:T(8,128)(2,1)S(1)}, bf16[1,512,2048]{2,1,0:T(8,128)(2,1)}, u32[]{:S(2)}) copy-start(bf16[1,512,2048]{2,1,0:T(8,128)(2,1)} %param.19) | copy-start | bytes 6291460
  6.5 288.4 %reduce-scatter.3.cloned.1.call-start = ((), (), s32[]{:S(2)}) async-start(), calls=%async_computation.5 | async-start | bytes 13369344 | tf_op jit(solution)/shard_map/reduce_scatter | solution.py:72
  36.7 148.5 %copy-start.6 = (f32[1,512]{1,0:T(1,128)S(1)}, f32[1,512]{1,0:T(1,128)}, u32[]{:S(2)}) copy-start(f32[1,512]{1,0:T(1,128)} %param.18) | copy-start | bytes 6148
  204.6 107.8 %copy-start.1 = (bf16[128,2048]{1,0:T(8,128)(2,1)S(1)}, bf16[128,2048]{1,0:T(8,128)(2,1)}, u32[]{:S(2)}) copy-start(bf16[128,2048]{1,0:T(8,128)(2,1)} %param.13) | copy-start | bytes 1572868
  204.7 108.2 %copy-start.2 = (f32[8,2048]{1,0:T(8,128)S(1)}, f32[8,2048]{1,0:T(8,128)}, u32[]{:S(2)}) copy-start(f32[8,2048]{1,0:T(8,128)} %param.20) | copy-start | bytes 196612
  204.7 109.6 %copy-start.3 = (f32[2048]{0:T(1024)S(1)}, f32[2048]{0:T(1024)}, u32[]{:S(2)}) copy-start(f32[2048]{0:T(1024)} %param.21) | copy-start | bytes 24580
  204.7 140.1 %all-gather.2.cloned.1.call-start = ((), (), s32[]{:S(2)}) async-start(), calls=%async_computation.6 | async-start | bytes 4718592 | tf_op jit(solution)/shard_map/all_gather | solution.py:94
  312.5 32.3 %copy-start.5 = (f32[1024]{0:T(1024)S(1)}, f32[1024]{0:T(1024)}, u32[]{:S(2)}) copy-start(f32[1024]{0:T(1024)} %param.23) | copy-start | bytes 12292
  315.3 81.9 %reduce-scatter.5.cloned.1.call-start = ((), (), s32[]{:S(2)}) async-start(), calls=%async_computation.7 | async-start | bytes 4718592 | tf_op jit(solution)/shard_map/reduce_scatter | solution.py:101
  359.1 38.1 %copy-start.4 = (f32[2048]{0:T(1024)S(1)}, f32[2048]{0:T(1024)}, u32[]{:S(2)}) copy-start(f32[2048]{0:T(1024)} %param.25) | copy-start | bytes 24580
Sparse Core Ops, SparseCore 0:
  204.8 90.1 reduce-scatter.2
  315.4 29.2 all-gather.1
  359.2 37.9 reduce-scatter.4
